TPU v7x, 256 devices: a whole 4x4x8 slice. The times are simulated.
256 devices in a mesh: ctx: 32 (over z, y), head: 8 (over x, core).
Axes of the slice: x: 4, y: 4, z: 8, core: 2. Of those that a mesh axis runs over, the one named last changes fastest.
Arguments:
- queries: bfloat16 [2048, 2048], P(None, 'head'), may hold values from -16 to 16
- prefix_keys: bfloat16 [32768, 2048], P('ctx', 'head'), may hold values from -6 to 6
- prefix_values: bfloat16 [32768, 2048], P('ctx', 'head'), may hold values from -6 to 6
- out_grad: bfloat16 [2048, 2048], P(None, 'head'), may hold values from -6 to 6
- block_lists: int32 [16, 16, 64], P('head'), may hold values from 0 to 511, as said below
- list_counts: int32 [16, 16], P('head'), may hold values from 32 to 64
Outputs:
- query_grad: bfloat16 [2048, 2048], P('ctx', 'head')
- key_grad: bfloat16 [32768, 2048], P(('ctx', 'head'))
- value_grad: bfloat16 [32768, 2048], P(('ctx', 'head'))
Inputs may be any that keep to these rules, and one draw needn't show every extreme that they name: `block_lists`: within a list all 64 entries are distinct block numbers; entries from list_counts on are ignored. Of the live entries of every list at most 8 lie in the blocks of one context slice (slice c holds blocks c * 16 onward), and exactly 8 in one slice.
All inputs are finite; a program needn't handle non-finite values.
Results may differ from a plain program's by a relative error of at most 0.017.
Values may be sent and summed in bfloat16 or wider, within the bound.
A program may use at most 128 MiB of HBM per device.

v0:
```python
import jax
import jax.numpy as jnp
from jax import lax
from jax.sharding import PartitionSpec as P

HD = 128
TILE = 128
BLOCK = 64
masked_score = -1e30


def joined(value, axis, join):
    pieces = jax.tree.map(lambda part: lax.all_gather(part, axis), value)
    head = jax.tree.map(lambda part: part[0], pieces)
    tail = jax.tree.map(lambda part: part[1:], pieces)
    running, _ = lax.scan(lambda running, piece: (join(running, piece), None), head, tail)
    return running


def pair_combine(former, latter):
    joint = jnp.maximum(former[0], latter[0])
    return (joint, former[1] * jnp.exp(former[0] - joint) + latter[1] * jnp.exp(latter[0] - joint))


def local(queries, prefix_keys, prefix_values, out_grad, block_lists, list_counts):
    heads_here = prefix_keys.shape[1] // HD
    slice_len = prefix_keys.shape[0]
    blocks_here = slice_len // BLOCK
    latents = queries.shape[0]
    score_scale = HD ** (-0.5)
    local_ids = block_lists - lax.axis_index("ctx") * blocks_here
    positions = jnp.arange(block_lists.shape[2], dtype=jnp.int32)
    listed = (
        (positions[None, None, :] < list_counts[:, :, None])
        & (local_ids >= 0)
        & (local_ids < blocks_here)
    )
    block_ids = jnp.arange(blocks_here, dtype=jnp.int32)
    chosen = jnp.any(listed[..., None] & (local_ids[..., None] == block_ids), axis=2)
    kept = []
    maxima = []
    totals = []
    for head_index in range(heads_here):
        first_col = head_index * HD
        query_head = queries[:, first_col : first_col + HD]
        key_head = prefix_keys[:, first_col : first_col + HD]
        value_head = prefix_values[:, first_col : first_col + HD]
        grad_head = out_grad[:, first_col : first_col + HD]
        key_mask = jnp.repeat(jnp.repeat(chosen[head_index], TILE, axis=0), BLOCK, axis=1)
        key_use = key_head
        value_use = value_head
        query_use = query_head
        grad_use = grad_head
        scores = score_scale * jnp.einsum(
            "ld,sd->ls", query_head, key_head, preferred_element_type=jnp.float32
        )
        dprobs = jnp.einsum("ld,sd->ls", grad_head, value_head, preferred_element_type=jnp.float32)
        scores = jnp.where(key_mask, scores, masked_score)
        row_max = jnp.max(scores, axis=-1)
        weights = jnp.where(key_mask, jnp.exp(scores - row_max[..., None]), 0.0)
        maxima.append(row_max)
        totals.append(jnp.sum(weights, axis=-1))
        kept.append((scores, dprobs, key_mask, key_use, value_use, query_use, grad_use))
    row_maxima = jnp.stack(maxima)
    row_totals = jnp.stack(totals)
    prob_list = []
    merged_max, merged_total = joined((row_maxima, row_totals), "ctx", pair_combine)
    log_totals = merged_max + jnp.log(merged_total)
    partial_deltas = []
    for head_index in range(heads_here):
        scores, dprobs, key_mask = (kept[head_index][0], kept[head_index][1], kept[head_index][2])
        log_here = log_totals[head_index][..., None]
        attn_probs = jnp.where(key_mask, jnp.exp(scores - log_here), 0.0)
        prob_list.append(attn_probs)
        partial_deltas.append(jnp.sum(attn_probs * dprobs, axis=-1))
    row_deltas = lax.psum(jnp.stack(partial_deltas), "ctx")
    query_terms = []
    key_terms = []
    value_terms = []
    for head_index in range(heads_here):
        scores, dprobs, key_mask, key_use, value_use, query_use, grad_use = kept[head_index]
        attn_probs = prob_list[head_index]
        delta_here = row_deltas[head_index][..., None]
        dscores = (attn_probs * (dprobs - delta_here)).astype(jnp.bfloat16)
        probs_low = attn_probs.astype(jnp.bfloat16)
        query_terms.append(
            score_scale
            * jnp.einsum("ls,sd->ld", dscores, key_use, preferred_element_type=jnp.float32)
        )
        key_terms.append(
            score_scale
            * jnp.einsum("ls,ld->sd", dscores, query_use, preferred_element_type=jnp.float32)
        )
        value_terms.append(
            jnp.einsum("ls,ld->sd", probs_low, grad_use, preferred_element_type=jnp.float32)
        )
    query_term = jnp.concatenate(query_terms, axis=1)
    key_local = jnp.concatenate(key_terms, axis=1).astype(jnp.bfloat16)
    value_local = jnp.concatenate(value_terms, axis=1).astype(jnp.bfloat16)
    own_rows = latents // lax.axis_size("ctx")
    summed = lax.psum(query_term, "ctx")
    query_grad = lax.dynamic_slice_in_dim(summed, lax.axis_index("ctx") * own_rows, own_rows, 0)
    key_grad, value_grad = (
        lax.all_to_all(key_local, "head", split_axis=0, concat_axis=1, tiled=True),
        lax.all_to_all(value_local, "head", split_axis=0, concat_axis=1, tiled=True),
    )
    return (query_grad.astype(jnp.bfloat16), key_grad, value_grad)


def solution(mesh):
    return jax.shard_map(
        local,
        mesh=mesh,
        in_specs=(
            P(None, "head"),
            P("ctx", "head"),
            P("ctx", "head"),
            P(None, "head"),
            P("head", None, None),
            P("head", None),
        ),
        out_specs=(P("ctx", "head"), P(("ctx", "head"), None), P(("ctx", "head"), None)),
        check_vma=False,
    )
```

profile of v0, /device:TPU:2, one launch (start us, length us, event | category | flops | bytes accessed | tf_op | source)
XLA Modules:
  0.0 488.2 jit_solution(2884194299780184191)
XLA Ops:
  0.7 0.9 fusion.39
  2.7 2.4 fusion.5
  5.1 1.3 fusion.4
  6.5 52.8 %all-gather.2 = f32[32,2,2048]{2,1,0:T(2,128)S(1)} all-gather(f32[1,2,2048]{2,1,0:T(2,128)S(1)} %maximum_bitcast_fusion), channel_id=2, replica_groups=mesh['ctx'=32,'head'=8] {'ctx'}, dimensions={0}, use_global_device_ids=true | all-gather | bytes 540672 | tf_op jit(solution)/shard_map/all_gather | solution.py:13
  59.4 2.1 fusion.3
  61.4 2.1 fusion.2
  63.5 48.3 %all-gather.3 = f32[32,2,2048]{2,1,0:T(2,128)S(1)} all-gather(f32[1,2,2048]{2,1,0:T(2,128)S(1)} %maximum_bitcast_fusion.1), channel_id=3, replica_groups=mesh['ctx'=32,'head'=8] {'ctx'}, dimensions={0}, use_global_device_ids=true | all-gather | bytes 540672 | tf_op jit(solution)/shard_map/all_gather | solution.py:13
  111.9 1.9 while.12
  113.9 9.2 %multiply_reduce_fusion = (f32[2048]{0:T(1024)S(1)}, f32[2048,1024]{0,1:T(8,128)}, f32[2048,1024]{0,1:T(8,128)}) fusion(f32[2048]{0:T(1024)S(1)} %bitcast.110, f32[2048,1024]{0,1:T(8,128)} %copy-done.1, pred[2048,16]{0,1:T(8,128)(4,1)S(1)} %bitcast.98, bf16[1024,256]{1,0:T(8,128)(2,1)} %param.10, bf16[2048,256]{1,0:T(8,128)(2,1)S(1)} %copy-done.3), kind=kOutput, calls=%fused_computation.15 | convolution fusion | flops 549451776 | bytes 26001408 | tf_op jit(solution)/shard_map/ld,sd->ls/dot_general | solution.py:57
  123.1 9.2 %multiply_reduce_fusion.1 = (f32[2048]{0:T(1024)S(1)}, f32[2048,1024]{0,1:T(8,128)}, f32[2048,1024]{0,1:T(8,128)}) fusion(f32[2048]{0:T(1024)S(1)} %bitcast.107, f32[2048,1024]{0,1:T(8,128)} %copy-done, pred[2048,16]{0,1:T(8,128)(4,1)S(1)} %bitcast.95, bf16[1024,256]{1,0:T(8,128)(2,1)S(1)} %copy-done.6, bf16[2048,256]{1,0:T(8,128)(2,1)S(1)} %copy-done.3), kind=kOutput, calls=%fused_computation.16 | convolution fusion | flops 549451776 | bytes 26001408 | tf_op jit(solution)/shard_map/ld,sd->ls/dot_general | solution.py:57
  132.2 140.5 %psum.14 = f32[2,2048]{1,0:T(2,128)S(1)} all-reduce(f32[2,2048]{1,0:T(2,128)S(1)} %pad_maximum_fusion.3), channel_id=1, replica_groups=mesh['ctx'=32,'head'=8] {'ctx'}, use_global_device_ids=true, to_apply=%region_9.10 | all-reduce | flops 4096 | bytes 32768 | tf_op jit(solution)/shard_map/psum | solution.py:76
  272.8 8.0 %multiply_convert_fusion = bf16[2048,1024]{0,1:T(8,128)(2,1)S(1)} fusion(f32[2048,1024]{0,1:T(8,128)} %get-tuple-element.57, f32[2048,1024]{0,1:T(8,128)} %get-tuple-element.70, f32[2048]{0:T(1024)S(1)} %bitcast.112), kind=kLoop, calls=%fused_computation.13 | loop fusion | flops 6291456 | bytes 20979712 | tf_op jit(solution)/shard_map/convert_element_type | solution.py:84
  280.8 2.7 fusion.17
  283.4 10.0 %multiply_convert_fusion.1 = bf16[2048,1024]{0,1:T(8,128)(2,1)} fusion(f32[2048,1024]{0,1:T(8,128)} %get-tuple-element.55, f32[2048,1024]{0,1:T(8,128)} %get-tuple-element.71, f32[2048]{0:T(1024)S(1)} %bitcast.109), kind=kLoop, calls=%fused_computation.14 | loop fusion | flops 6291456 | bytes 20979712 | tf_op jit(solution)/shard_map/convert_element_type | solution.py:84
  293.4 3.5 fusion.16
  297.8 4.8 all-to-all-start
  302.6 3.0 convolution_multiply_fusion
  305.6 3.1 convolution_multiply_fusion.1
  308.7 4.8 fusion.13
  313.7 1.2 fusion.10
  315.8 4.8 all-to-all-start.1
  320.7 163.2 %all-reduce.1 = bf16[2048,256]{0,1:T(8,128)(2,1)} all-reduce(f32[2048,256]{0,1:T(8,128)S(1)} %pad_maximum_fusion), channel_id=1, replica_groups=mesh['ctx'=32,'head'=8] {'ctx'}, use_global_device_ids=true, to_apply=%region_10.11 | all-reduce | flops 524288 | bytes 3145728 | tf_op jit(solution)/shard_map/psum | solution.py:101
  483.8 0.9 dynamic-slice_convert_fusion
  485.5 1.9 copy.20
  (75 shorter events, 6.3 us)
Async XLA Ops:
  0.6 4.5 copy-start.4
  0.6 4.5 copy-start.5
  5.1 56.3 %copy-start.1 = (f32[2048,1024]{0,1:T(8,128)}, f32[2048,1024]{0,1:T(8,128)S(1)}, u32[]{:S(2)}) copy-start(f32[2048,1024]{0,1:T(8,128)S(1)} %get-tuple-element.67) | copy-start | bytes 25165828
  6.5 57.0 %copy-start = (f32[2048,1024]{0,1:T(8,128)}, f32[2048,1024]{0,1:T(8,128)S(1)}, u32[]{:S(2)}) copy-start(f32[2048,1024]{0,1:T(8,128)S(1)} %get-tuple-element.69) | copy-start | bytes 25165828
  59.3 54.5 %copy-start.3 = (bf16[2048,256]{1,0:T(8,128)(2,1)S(1)}, bf16[2048,256]{1,0:T(8,128)(2,1)}, u32[]{:S(2)}) copy-start(bf16[2048,256]{1,0:T(8,128)(2,1)} %param.11) | copy-start | bytes 3145732
  113.8 9.2 %copy-start.6 = (bf16[1024,256]{1,0:T(8,128)(2,1)S(1)}, bf16[1024,256]{1,0:T(8,128)(2,1)}, u32[]{:S(2)}) copy-start(bf16[1024,256]{1,0:T(8,128)(2,1)} %param.10) | copy-start | bytes 1572868
  280.8 12.6 %copy-start.2 = (bf16[2048,1024]{0,1:T(8,128)(2,1)}, bf16[2048,1024]{0,1:T(8,128)(2,1)S(1)}, u32[]{:S(2)}) copy-start(bf16[2048,1024]{0,1:T(8,128)(2,1)S(1)} %multiply_convert_fusion) | copy-start | bytes 12582916
  297.8 18.0 %all-to-all-start = ((bf16[8,128,256]{2,1,0:T(8,128)(2,1)}), bf16[8,128,256]{2,1,0:T(8,128)(2,1)}, u32[]{:S(2)}, u32[]{:S(2)}) async-start(bf16[8,128,256]{2,1,0:T(8,128)(2,1)} %pad_maximum_fusion.1), calls=%async_computation | async-start | bytes 1048576 | tf_op jit(solution)/shard_map/all_to_all | solution.py:104
  305.6 8.1 %slice-start = ((s8[8388608]{0:T(1024)(128)(4,1)}), s8[4194304]{0:T(1024)(128)(4,1)S(1)}, s32[]{:S(2)}) async-start(s8[8388608]{0:T(1024)(128)(4,1)} %bitcast.88), calls=%async_computation.2 | async-start | bytes 8388608
  308.7 5.0 %slice-start.1 = ((s8[8388608]{0:T(1024)(128)(4,1)}), s8[4194304]{0:T(1024)(128)(4,1)S(1)}, s32[]{:S(2)}) async-start(s8[8388608]{0:T(1024)(128)(4,1)} %bitcast.88), calls=%async_computation.3 | async-start | bytes 8388608
  315.8 171.5 %all-to-all-start.1 = ((bf16[8,128,256]{2,1,0:T(8,128)(2,1)}), bf16[8,128,256]{2,1,0:T(8,128)(2,1)S(1)}, u32[]{:S(2)}, u32[]{:S(2)}) async-start(bf16[8,128,256]{2,1,0:T(8,128)(2,1)} %pad_maximum_fusion.2), calls=%async_computation.1 | async-start | bytes 1048576 | tf_op jit(solution)/shard_map/all_to_all | solution.py:105
where the time goes:
time: 489 us; the launch traced here: 488 us
  blocking collectives  405 us (83%)
  matrix products  40.4 us (8%)
  other arithmetic  27.1 us (6%)
  starting transfers between devices  9.64 us (2%)
  local copies, waits for them, and re-layouts  4.93 us (1%)
    psum x1, blocking collectives, local(): summed = lax.psum(query_term, 'ctx')  163 us
    psum x1, blocking collectives, local(): row_deltas = lax.psum(jnp.stack(partial_deltas), 'ctx')  141 us
    all_gather x2, blocking collectives, joined(): pieces = jax.tree.map(lambda part: lax.all_gather(part, axis), value)  101 us
    dot_general x2, matrix products, local(): jnp.einsum('ld,sd->ls', grad_head, value_head, preferred_element_type=jnp...  18.4 us
    convert_element_type x2, other arithmetic, local(): dscores = (attn_probs * (dprobs - delta_here)).astype(jnp.bfloat16)  17.9 us
  transfers between devices with their start and end apart: 2, of which 0 were waited for; matrix products, arithmetic and copies ran while one was open for 3% of the time, Pallas kernels for 0%

commit v1 on v0

--- a/solution.py
+++ b/solution.py
@@ -98,7 +98,9 @@
     key_local = jnp.concatenate(key_terms, axis=1).astype(jnp.bfloat16)
     value_local = jnp.concatenate(value_terms, axis=1).astype(jnp.bfloat16)
     own_rows = latents // lax.axis_size("ctx")
-    summed = lax.psum(query_term, "ctx")
+    summed = query_term
+    for hop in (1, 2, 4, 8, 16):
+        summed = summed + lax.ppermute(summed, "ctx", [(dev, dev ^ hop) for dev in range(32)])
     query_grad = lax.dynamic_slice_in_dim(summed, lax.axis_index("ctx") * own_rows, own_rows, 0)
     key_grad, value_grad = (
         lax.all_to_all(key_local, "head", split_axis=0, concat_axis=1, tiled=True),

time: 489 us -> 540 us (1.10)
  waiting for transfers between devices: 0.01 us -> 211 us
  blocking collectives: 405 us -> 242 us
    ppermute x0 -> x5, waiting for transfers between devices: none -> 203 us  [local(): lax.ppermute(summed, 'ctx', [(dev, dev ^ hop) for dev in range(32)])]
    psum x1 -> x0, blocking collectives: 163 us -> none  [local(): summed = lax.psum(query_term, 'ctx')]
    all_to_all x1, waiting for transfers between devices: 0.01 us -> 8.05 us  [local(): lax.all_to_all(value_local, 'head', split_axis=0, concat_axis=1, tiled=True)]
  transfers between devices with their start and end apart: 2 -> 7, of which waited for: 0 -> 6; matrix products, arithmetic and copies ran while one was open for 3% -> 3% of each run, Pallas kernels for 0% -> 0%
where the time goes in v1:
time: 540 us
  blocking collectives  242 us (45%)
  waiting for transfers between devices  211 us (39%)
  matrix products  38.5 us (7%)
  other arithmetic  30.8 us (6%)
  starting transfers between devices  13.4 us (2%)
    ppermute x5, waiting for transfers between devices, local(): lax.ppermute(summed, 'ctx', [(dev, dev ^ hop) for dev in range(32)])  203 us
    psum x1, blocking collectives, local(): row_deltas = lax.psum(jnp.stack(partial_deltas), 'ctx')  141 us
    all_gather x2, blocking collectives, joined(): pieces = jax.tree.map(lambda part: lax.all_gather(part, axis), value)  101 us
    dot_general x2, matrix products, local(): jnp.einsum('ld,sd->ls', grad_head, value_head, preferred_element_type=jnp...  18.3 us
    convert_element_type x2, other arithmetic, local(): dscores = (attn_probs * (dprobs - delta_here)).astype(jnp.bfloat16)  17.9 us
  transfers between devices with their start and end apart: 7, of which 6 were waited for; matrix products, arithmetic and copies ran while one was open for 3% of the time, Pallas kernels for 0%

profile of v1, /device:TPU:2, one launch (start us, length us, event | category | flops | bytes accessed | tf_op | source)
XLA Modules:
  0.0 539.9 jit_solution(12304093968775266587)
XLA Ops:
  2.7 2.4 fusion.5
  6.5 52.8 %all-gather.2 = f32[32,2,2048]{2,1,0:T(2,128)S(1)} all-gather(f32[1,2,2048]{2,1,0:T(2,128)S(1)} %maximum_bitcast_fusion), channel_id=2, replica_groups=mesh['ctx'=32,'head'=8] {'ctx'}, dimensions={0}, use_global_device_ids=true | all-gather | bytes 540672 | tf_op jit(solution)/shard_map/all_gather | solution.py:13
  59.4 2.1 fusion.3
  61.4 2.1 fusion.2
  63.5 48.3 %all-gather.3 = f32[32,2,2048]{2,1,0:T(2,128)S(1)} all-gather(f32[1,2,2048]{2,1,0:T(2,128)S(1)} %maximum_bitcast_fusion.1), channel_id=3, replica_groups=mesh['ctx'=32,'head'=8] {'ctx'}, dimensions={0}, use_global_device_ids=true | all-gather | bytes 540672 | tf_op jit(solution)/shard_map/all_gather | solution.py:13
  111.9 1.9 while.12
  113.9 9.2 %multiply_reduce_fusion = (f32[2048]{0:T(1024)S(1)}, f32[2048,1024]{0,1:T(8,128)}, f32[2048,1024]{0,1:T(8,128)}) fusion(f32[2048]{0:T(1024)S(1)} %bitcast.109, f32[2048,1024]{0,1:T(8,128)} %copy-done.1, pred[2048,16]{0,1:T(8,128)(4,1)S(1)} %bitcast.97, bf16[1024,256]{1,0:T(8,128)(2,1)S(1)} %copy-done.7, bf16[2048,256]{1,0:T(8,128)(2,1)S(1)} %copy-done.3), kind=kOutput, calls=%fused_computation.15 | convolution fusion | flops 549451776 | bytes 26001408 | tf_op jit(solution)/shard_map/ld,sd->ls/dot_general | solution.py:57
  123.0 9.1 %multiply_reduce_fusion.1 = (f32[2048]{0:T(1024)S(1)}, f32[2048,1024]{0,1:T(8,128)}, f32[2048,1024]{0,1:T(8,128)}) fusion(f32[2048]{0:T(1024)S(1)} %bitcast.106, f32[2048,1024]{0,1:T(8,128)} %copy-done, pred[2048,16]{0,1:T(8,128)(4,1)S(1)} %bitcast.94, bf16[1024,256]{1,0:T(8,128)(2,1)S(1)} %copy-done.7, bf16[2048,256]{1,0:T(8,128)(2,1)S(1)} %copy-done.3), kind=kOutput, calls=%fused_computation.16 | convolution fusion | flops 549451776 | bytes 26001408 | tf_op jit(solution)/shard_map/ld,sd->ls/dot_general | solution.py:57
  132.2 140.5 %psum.7 = f32[2,2048]{1,0:T(2,128)S(1)} all-reduce(f32[2,2048]{1,0:T(2,128)S(1)} %pad_maximum_fusion.3), channel_id=1, replica_groups=mesh['ctx'=32,'head'=8] {'ctx'}, use_global_device_ids=true, to_apply=%region_9.10 | all-reduce | flops 4096 | bytes 32768 | tf_op jit(solution)/shard_map/psum | solution.py:76
  272.7 8.0 %multiply_convert_fusion = bf16[2048,1024]{0,1:T(8,128)(2,1)S(1)} fusion(f32[2048,1024]{0,1:T(8,128)} %get-tuple-element.57, f32[2048,1024]{0,1:T(8,128)} %get-tuple-element.70, f32[2048]{0:T(1024)S(1)} %bitcast.111), kind=kLoop, calls=%fused_computation.13 | loop fusion | flops 6291456 | bytes 20979712 | tf_op jit(solution)/shard_map/convert_element_type | solution.py:84
  280.7 1.7 convolution_multiply_fusion
  282.4 9.9 %multiply_convert_fusion.1 = bf16[2048,1024]{0,1:T(8,128)(2,1)} fusion(f32[2048,1024]{0,1:T(8,128)} %get-tuple-element.55, f32[2048,1024]{0,1:T(8,128)} %get-tuple-element.71, f32[2048]{0:T(1024)S(1)} %bitcast.108), kind=kLoop, calls=%fused_computation.14 | loop fusion | flops 6291456 | bytes 20979712 | tf_op jit(solution)/shard_map/convert_element_type | solution.py:84
  292.4 3.0 convolution_multiply_fusion.1
  295.6 26.0 %collective-permute-done = f32[2048,256]{0,1:T(8,128)S(1)} collective-permute-done((f32[2048,256]{0,1:T(8,128)S(1)}, f32[2048,256]{0,1:T(8,128)S(1)}, u32[]{:S(2)}, u32[]{:S(2)}) %collective-permute-start) | collective-permute-done | bytes 2097184 | tf_op jit(solution)/shard_map/ppermute | solution.py:103
  322.1 27.5 %collective-permute-done.1 = f32[2048,256]{0,1:T(8,128)S(1)} collective-permute-done((f32[2048,256]{0,1:T(8,128)S(1)}, f32[2048,256]{0,1:T(8,128)S(1)}, u32[]{:S(2)}, u32[]{:S(2)}) %collective-permute-start.1) | collective-permute-done | bytes 2097184 | tf_op jit(solution)/shard_map/ppermute | solution.py:103
  350.1 84.4 %collective-permute-done.2 = f32[2048,256]{0,1:T(8,128)S(1)} collective-permute-done((f32[2048,256]{0,1:T(8,128)S(1)}, f32[2048,256]{0,1:T(8,128)S(1)}, u32[]{:S(2)}, u32[]{:S(2)}) %collective-permute-start.2) | collective-permute-done | bytes 2097184 | tf_op jit(solution)/shard_map/ppermute | solution.py:103
  435.0 48.9 %collective-permute-done.3 = f32[2048,256]{0,1:T(8,128)S(1)} collective-permute-done((f32[2048,256]{0,1:T(8,128)S(1)}, f32[2048,256]{0,1:T(8,128)S(1)}, u32[]{:S(2)}, u32[]{:S(2)}) %collective-permute-start.3) | collective-permute-done | bytes 2097184 | tf_op jit(solution)/shard_map/ppermute | solution.py:103
  485.4 3.4 collective-permute-start.4
  492.2 4.8 all-to-all-start
  497.0 4.6 fusion.13
  501.6 4.6 fusion.10
  507.1 4.8 all-to-all-start.1
  512.8 8.0 %all-to-all-done.1 = bf16[8,128,256]{2,1,0:T(8,128)(2,1)S(1)} async-done(((bf16[8,128,256]{2,1,0:T(8,128)(2,1)}), bf16[8,128,256]{2,1,0:T(8,128)(2,1)S(1)}, u32[]{:S(2)}, u32[]{:S(2)}) %all-to-all-start.1) | async-done | bytes 524320 | tf_op jit(solution)/shard_map/all_to_all | solution.py:107
  521.7 16.4 %collective-permute-done.4 = f32[2048,256]{0,1:T(8,128)} collective-permute-done((f32[2048,256]{0,1:T(8,128)}, f32[2048,256]{0,1:T(8,128)}, u32[]{:S(2)}, u32[]{:S(2)}) %collective-permute-start.4) | collective-permute-done | bytes 2097184 | tf_op jit(solution)/shard_map/ppermute | solution.py:103
  (85 shorter events, 15.9 us)
Async XLA Ops:
  0.6 4.5 copy-start.4
  0.6 4.5 copy-start.5
  5.1 56.3 %copy-start.1 = (f32[2048,1024]{0,1:T(8,128)}, f32[2048,1024]{0,1:T(8,128)S(1)}, u32[]{:S(2)}) copy-start(f32[2048,1024]{0,1:T(8,128)S(1)} %get-tuple-element.67) | copy-start | bytes 25165828
  6.5 57.0 %copy-start = (f32[2048,1024]{0,1:T(8,128)}, f32[2048,1024]{0,1:T(8,128)S(1)}, u32[]{:S(2)}) copy-start(f32[2048,1024]{0,1:T(8,128)S(1)} %get-tuple-element.69) | copy-start | bytes 25165828
  59.3 54.5 %copy-start.3 = (bf16[2048,256]{1,0:T(8,128)(2,1)S(1)}, bf16[2048,256]{1,0:T(8,128)(2,1)}, u32[]{:S(2)}) copy-start(bf16[2048,256]{1,0:T(8,128)(2,1)} %param.11) | copy-start | bytes 3145732
  59.4 54.5 %copy-start.7 = (bf16[1024,256]{1,0:T(8,128)(2,1)S(1)}, bf16[1024,256]{1,0:T(8,128)(2,1)}, u32[]{:S(2)}) copy-start(bf16[1024,256]{1,0:T(8,128)(2,1)} %param.10) | copy-start | bytes 1572868
  295.5 26.1 %collective-permute-start = (f32[2048,256]{0,1:T(8,128)S(1)}, f32[2048,256]{0,1:T(8,128)S(1)}, u32[]{:S(2)}, u32[]{:S(2)}) collective-permute-start(f32[2048,256]{0,1:T(8,128)S(1)} %pad_maximum_fusion), channel_id=1, source_target_pairs={{0,8},{8,0},{16,24},{24,16},{32,40},{40,32},{48,56},{56,48},{64,72... | collective-permute-start | bytes 6291464 | tf_op jit(solution)/shard_map/ppermute | solution.py:103
  322.0 166.8 %copy-start.6 = (bf16[2048,256]{1,0:T(8,128)(2,1)S(1)}, bf16[2048,256]{1,0:T(8,128)(2,1)}, u32[]{:S(2)}) copy-start(bf16[2048,256]{1,0:T(8,128)(2,1)} %param.8) | copy-start | bytes 3145732
  322.0 27.6 %collective-permute-start.1 = (f32[2048,256]{0,1:T(8,128)S(1)}, f32[2048,256]{0,1:T(8,128)S(1)}, u32[]{:S(2)}, u32[]{:S(2)}) collective-permute-start(f32[2048,256]{0,1:T(8,128)S(1)} %fusion.41), channel_id=1, source_target_pairs={{0,16},{8,24},{16,0},{24,8},{32,48},{40,56},{48,32},{56,40},{64,80... | collective-permute-start | bytes 6291464 | tf_op jit(solution)/shard_map/ppermute | solution.py:103
  350.0 140.1 %copy-start.2 = (bf16[2048,1024]{0,1:T(8,128)(2,1)S(1)}, bf16[2048,1024]{0,1:T(8,128)(2,1)}, u32[]{:S(2)}) copy-start(bf16[2048,1024]{0,1:T(8,128)(2,1)} %multiply_convert_fusion.1) | copy-start | bytes 12582916
  350.0 84.5 %collective-permute-start.2 = (f32[2048,256]{0,1:T(8,128)S(1)}, f32[2048,256]{0,1:T(8,128)S(1)}, u32[]{:S(2)}, u32[]{:S(2)}) collective-permute-start(f32[2048,256]{0,1:T(8,128)S(1)} %add.31), channel_id=1, source_target_pairs={{0,32},{8,40},{16,48},{24,56},{32,0},{40,8},{48,16},{56,24},{64,96... | collective-permute-start | bytes 6291464 | tf_op jit(solution)/shard_map/ppermute | solution.py:103
  434.9 49.0 %collective-permute-start.3 = (f32[2048,256]{0,1:T(8,128)S(1)}, f32[2048,256]{0,1:T(8,128)S(1)}, u32[]{:S(2)}, u32[]{:S(2)}) collective-permute-start(f32[2048,256]{0,1:T(8,128)S(1)} %add.32), channel_id=1, source_target_pairs={{0,64},{8,72},{16,80},{24,88},{32,96},{40,104},{48,112},{56,120},{... | collective-permute-start | bytes 6291464 | tf_op jit(solution)/shard_map/ppermute | solution.py:103
  485.4 52.7 %collective-permute-start.4 = (f32[2048,256]{0,1:T(8,128)}, f32[2048,256]{0,1:T(8,128)}, u32[]{:S(2)}, u32[]{:S(2)}) collective-permute-start(f32[2048,256]{0,1:T(8,128)} %add.33), channel_id=1, source_target_pairs={{0,128},{8,136},{16,144},{24,152},{32,160},{40,168},{48,176},{56,1... | collective-permute-start | bytes 6291464 | tf_op jit(solution)/shard_map/ppermute | solution.py:103
  492.2 14.9 %all-to-all-start = ((bf16[8,128,256]{2,1,0:T(8,128)(2,1)}), bf16[8,128,256]{2,1,0:T(8,128)(2,1)S(1)}, u32[]{:S(2)}, u32[]{:S(2)}) async-start(bf16[8,128,256]{2,1,0:T(8,128)(2,1)} %pad_maximum_fusion.1), calls=%async_computation | async-start | bytes 1048576 | tf_op jit(solution)/shard_map/all_to_all | solution.py:106
  507.1 13.7 %all-to-all-start.1 = ((bf16[8,128,256]{2,1,0:T(8,128)(2,1)}), bf16[8,128,256]{2,1,0:T(8,128)(2,1)S(1)}, u32[]{:S(2)}, u32[]{:S(2)}) async-start(bf16[8,128,256]{2,1,0:T(8,128)(2,1)} %pad_maximum_fusion.2), calls=%async_computation.1 | async-start | bytes 1048576 | tf_op jit(solution)/shard_map/all_to_all | solution.py:107
